TPU v7x, 512 devices: a whole 4x4x16 slice. The times are simulated.
512 devices in a mesh: gz: 128 (over z, y, core), row: 4 (over x).
Axes of the slice: x: 4, y: 4, z: 16, core: 2. Of those that a mesh axis runs over, the one named last changes fastest.
Arguments:
- tokens: bfloat16 [262144, 384], P(('gz', 'row')), may hold values from -6 to 6
- key_blocks: int32 [4096, 20], P(('gz', 'row')), may hold values from 0 to 4095, as said below
- counts: int32 [128], replicated, may hold values from 8 to 32, as said below
- norm_gain: float32 [384], replicated, may hold values from 0.1 to 1.9
- qkv_weight: bfloat16 [384, 1152], replicated, may hold values from -1 to 1
- out_weight: bfloat16 [384, 384], replicated, may hold values from -0.3125 to 0.3125
- mlp_gain: float32 [384], replicated, may hold values from 0.1 to 1.9
- up_weight: bfloat16 [384, 1536], replicated, may hold values from -0.3125 to 0.3125
- down_weight: bfloat16 [1536, 384], replicated, may hold values from -0.15625 to 0.15625
Outputs:
- block_out: bfloat16 [262144, 384], P(('gz', 'row'))
Inputs may be any that keep to these rules, and one draw needn't show every extreme that they name: `key_blocks`: entries 0 to 3 of a query block's list name live blocks of the query's own slab (repeats possible). The other 16 entries name blocks with the same row group as the query block (id % 32 // 8 equal), in any slab; over the blocks of one device each slab is named by exactly 1 such entries. `counts`: one slab is full in every draw.
All inputs are finite; a program needn't handle non-finite values.
Results may differ from a plain program's by a relative error of at most 0.01.
Values may be sent and summed in bfloat16 or wider, within the bound.
A program may use at most 128 MiB of HBM per device.

v0:
```python
import jax
import jax.numpy as jnp
from jax import lax
from jax.sharding import PartitionSpec as P

H = 12
NNEAR = 4
NFAR = 16


def rms_norm(values, gain):
    mean_sq = jnp.mean(values * values, axis=-1, keepdims=True)
    return values * lax.rsqrt(mean_sq + 1e-05) * gain


def attend(query_block, key_values, live_blocks):
    model_width = query_block.shape[1]
    head_size = model_width // H
    keys = key_values[:, :, :model_width].reshape(-1, H, head_size)
    values = key_values[:, :, model_width:].reshape(-1, H, head_size)
    heads = query_block.reshape(-1, H, head_size)
    scores = jnp.einsum("qhd,khd->hqk", heads, keys, preferred_element_type=jnp.float32) / jnp.sqrt(
        jnp.float32(head_size)
    )
    key_live = jnp.repeat(live_blocks, key_values.shape[1])
    scores = jnp.where(key_live[None, None, :], scores, jnp.float32(-1e30))
    top = jnp.max(scores, axis=-1, keepdims=True)
    weights = jnp.exp(scores - top)
    total = jnp.sum(weights, axis=-1)
    mixed = jnp.einsum(
        "hqk,khd->qhd", weights.astype(jnp.bfloat16), values, preferred_element_type=jnp.float32
    )
    mixed = mixed / jnp.transpose(total)[:, :, None]
    return mixed.reshape(-1, model_width).astype(jnp.bfloat16)


def body(
    tokens, key_blocks, counts, norm_gain, qkv_weight, out_weight, mlp_gain, up_weight, down_weight
):
    model_width = tokens.shape[1]
    own_blocks = key_blocks.shape[0]
    block_len = tokens.shape[0] // own_blocks
    slabs_n = lax.axis_size("gz")
    slab_blocks = own_blocks * lax.axis_size("row")
    inputs = tokens.astype(jnp.float32)
    normed = rms_norm(inputs, norm_gain).astype(jnp.bfloat16)
    projected = jnp.dot(normed, qkv_weight, preferred_element_type=jnp.float32).astype(jnp.bfloat16)
    queries = projected[:, :model_width].reshape(own_blocks, block_len, model_width)
    kv_own = projected[:, model_width:].reshape(own_blocks, block_len, 2 * model_width)
    slab_kv = lax.all_gather(kv_own, "row", axis=0, tiled=True)
    owner_slab = key_blocks // slab_blocks
    within = key_blocks % slab_blocks
    slab_table = jnp.arange(slabs_n, dtype=jnp.int32)
    slab_count = jnp.sum(jnp.where(owner_slab[:, :, None] == slab_table, counts, 0), axis=-1)
    live = within < slab_count
    near_rows = within[:, :NNEAR]
    far_owner = owner_slab[:, NNEAR:].reshape(-1)
    far_local = (key_blocks[:, NNEAR:] % own_blocks).reshape(-1)
    request_count = far_owner.shape[0]
    per_owner = request_count // slabs_n
    slab_hits = (far_owner[:, None] == slab_table[None, :]).astype(jnp.int32)
    slot_rank = jnp.sum((jnp.cumsum(slab_hits, axis=0) - 1) * slab_hits, axis=1)
    far_slot = far_owner * per_owner + slot_rank
    slot_hits = far_slot[:, None] == jnp.arange(request_count, dtype=jnp.int32)[None, :]
    request = jnp.sum(jnp.where(slot_hits, far_local[:, None], 0), axis=0)
    wanted = lax.all_to_all(
        request.reshape(slabs_n, per_owner), "gz", split_axis=0, concat_axis=0, tiled=True
    ).reshape(-1)
    kv_sent = kv_own[wanted].reshape(slabs_n, per_owner, block_len, 2 * model_width)
    far_kv = lax.all_to_all(kv_sent, "gz", split_axis=0, concat_axis=0, tiled=True).reshape(
        request_count, block_len, 2 * model_width
    )
    far_slots = far_slot.reshape(own_blocks, NFAR)

    def one_block(packed):
        query_block, near_row, slot_row, live_blocks = packed
        gathered = jnp.concatenate([slab_kv[near_row], far_kv[slot_row]], axis=0)
        return attend(query_block, gathered, live_blocks)

    attended = lax.map(one_block, (queries, near_rows, far_slots, live)).reshape(-1, model_width)
    residual = (inputs + jnp.dot(attended, out_weight, preferred_element_type=jnp.float32)).astype(
        jnp.bfloat16
    )
    normed_two = rms_norm(residual.astype(jnp.float32), mlp_gain).astype(jnp.bfloat16)
    hidden = jax.nn.gelu(jnp.dot(normed_two, up_weight, preferred_element_type=jnp.float32)).astype(
        jnp.bfloat16
    )
    result = residual.astype(jnp.float32) + jnp.dot(
        hidden, down_weight, preferred_element_type=jnp.float32
    )
    return result.astype(jnp.bfloat16)


def solution(mesh):
    return jax.shard_map(
        body,
        mesh=mesh,
        in_specs=(
            P(("gz", "row"), None),
            P(("gz", "row"), None),
            P(),
            P(),
            P(),
            P(),
            P(),
            P(),
            P(),
        ),
        out_specs=P(("gz", "row"), None),
        check_vma=False,
    )
```

profile of v0, /device:TPU:34, one launch (start us, length us, event | category | flops | bytes accessed | tf_op | source)
XLA Modules:
  0.0 899.9 jit_solution(1121670228715320951)
XLA Ops:
  9.8 19.2 %all-to-all-start = ((s32[128,1,1]{2,1,0:T(1,128)}), s32[128,1,1]{2,1,0:T(1,128)S(1)}, u32[]{:S(2)}, u32[]{:S(2)}) async-start(s32[128,1,1]{2,1,0:T(1,128)} %copy.50), calls=%async_computation | async-start | bytes 131072 | tf_op jit(solution)/shard_map/all_to_all | solution.py:66
  33.1 10.2 %all-to-all-done = s32[128,1,1]{2,1,0:T(1,128)S(1)} async-done(((s32[128,1,1]{2,1,0:T(1,128)}), s32[128,1,1]{2,1,0:T(1,128)S(1)}, u32[]{:S(2)}, u32[]{:S(2)}) %all-to-all-start) | async-done | bytes 544 | tf_op jit(solution)/shard_map/all_to_all | solution.py:66
  45.6 8.3 gather_fusion.2
  53.9 7.6 all-to-all-start.1
  65.7 46.3 %all-gather.2.cloned.1.call-done = bf16[32,64,768]{2,1,0:T(8,128)(2,1)} async-done(((bf16[8,64,768]{2,1,0:T(8,128)(2,1)}), bf16[32,64,768]{2,1,0:T(8,128)(2,1)}) %all-gather.2.cloned.1.call-update) | async-done | bytes 3145744 | tf_op jit(solution)/shard_map/all_gather | solution.py:50
  112.0 496.7 %all-to-all-done.1 = bf16[128,1,64,768]{3,2,1,0:T(8,128)(2,1)} async-done(((bf16[128,1,64,768]{3,2,1,0:T(8,128)(2,1)}), bf16[128,1,64,768]{3,2,1,0:T(8,128)(2,1)}, u32[]{:S(2)}, u32[]{:S(2)}) %all-to-all-start.1) | async-done | bytes 12582944 | tf_op jit(solution)/shard_map/all_to_all | solution.py:70
  608.7 278.2 %while.10 = (s32[]{:T(128)}, bf16[8,64,384]{2,1,0:T(8,128)(2,1)}, s32[8,4]{1,0:T(8,128)}, bf16[32,64,768]{2,1,0:T(8,128)(2,1)}, s32[8,16]{1,0:T(8,128)}, /*index...) while((s32[]{:T(128)}, bf16[8,64,384]{2,1,0:T(8,128)(2,1)}, ...), condition=%wide.region_8.9_spmd, body=%wide.region_5.8_spmd.sunk | while | flops 132760128 | bytes 49673220 | solution.py:80
  613.4 5.2 gather_fusion.1
  639.6 3.1 fusion.79
  648.1 5.2 gather_fusion.1
  674.4 3.1 fusion.79
  682.9 5.2 gather_fusion.1
  709.2 3.1 fusion.79
  717.7 5.2 gather_fusion.1
  743.9 3.1 fusion.79
  752.5 5.2 gather_fusion.1
  778.7 3.1 fusion.79
  787.2 5.2 gather_fusion.1
  813.5 3.1 fusion.79
  822.0 5.2 gather_fusion.1
  848.3 3.1 fusion.79
  856.8 5.2 gather_fusion.1
  883.0 3.1 fusion.79
  888.6 3.5 fusion.29
  (221 shorter events, 227.2 us)
Async XLA Ops:
  6.5 882.0 %copy-start = (bf16[1536,384]{1,0:T(8,128)(2,1)S(1)}, bf16[1536,384]{1,0:T(8,128)(2,1)}, u32[]{:S(2)}) copy-start(bf16[1536,384]{1,0:T(8,128)(2,1)} %param.19) | copy-start | bytes 3538948
  9.8 33.5 %all-to-all-start = ((s32[128,1,1]{2,1,0:T(1,128)}), s32[128,1,1]{2,1,0:T(1,128)S(1)}, u32[]{:S(2)}, u32[]{:S(2)}) async-start(s32[128,1,1]{2,1,0:T(1,128)} %copy.50), calls=%async_computation | async-start | bytes 131072 | tf_op jit(solution)/shard_map/all_to_all | solution.py:66
  30.1 0.8 copy-start.3
  33.1 20.9 %copy-start.2 = (bf16[512,768]{1,0:T(8,128)(2,1)}, bf16[512,768]{1,0:T(8,128)(2,1)S(1)}, u32[]{:S(2)}) copy-start(bf16[512,768]{1,0:T(8,128)(2,1)S(1)} %slice.35) | copy-start | bytes 2359300
  53.9 10.0 %copy-start.4 = (s32[128]{0:T(128)S(1)}, s32[128]{0:T(128)}, u32[]{:S(2)}) copy-start(s32[128]{0:T(128)} %param.13) | copy-start | bytes 1540
  53.9 554.8 %all-to-all-start.1 = ((bf16[128,1,64,768]{3,2,1,0:T(8,128)(2,1)}), bf16[128,1,64,768]{3,2,1,0:T(8,128)(2,1)}, u32[]{:S(2)}, u32[]{:S(2)}) async-start(bf16[128,1,64,768]{3,2,1,0:T(8,128)(2,1)} %bitcast.77), calls=%async_computation.1 | async-start | bytes 25165824 | tf_op jit(solution)/shard_map/all_to_all | solution.py:70
  61.5 50.5 %all-gather.2.cloned.1.call-start = ((), (), s32[]{:S(2)}) async-start(), calls=%async_computation.2 | async-start | bytes 3932160 | tf_op jit(solution)/shard_map/all_gather | solution.py:50
  631.8 1.9 copy-start.1
  666.6 1.9 copy-start.1
  701.4 1.9 copy-start.1
  736.2 1.9 copy-start.1
  770.9 1.9 copy-start.1
  805.7 1.9 copy-start.1
  840.5 1.9 copy-start.1
  875.3 1.9 copy-start.1
Sparse Core Ops, SparseCore 0:
  64.5 47.5 all-gather.1
where the time goes:
time: 903 us; the launch traced here: 900 us
  waiting for transfers between devices  554 us (61%)
  local copies, waits for them, and re-layouts  236 us (26%)
  matrix products  48.5 us (5%)
  starting transfers between devices  27 us (3%)
  other arithmetic  21.2 us (2%)
  between operations  13.5 us (1%)
    all_to_all x1, waiting for transfers between devices, body(): lax.all_to_all(kv_sent, 'gz', split_axis=0, concat_axis=0, tiled=True)  497 us
    gather x16, local copies, waits for them, and re-layouts, one_block(): gathered = jnp.concatenate([slab_kv[near_row], far_kv[slot_row]], axis=0)  61.5 us
    all_gather x1, waiting for transfers between devices, body(): slab_kv = lax.all_gather(kv_own, 'row', axis=0, tiled=True)  46.3 us
    slice x16, local copies, waits for them, and re-layouts, attend(): keys = key_values[:, :, :model_width].reshape(-1, H, head_size)  46.1 us
    dot_general x8, matrix products, attend(): jnp.einsum('hqk,khd->qhd', weights.astype(jnp.bfloat16), values, preferre...  25.1 us
    slice x8, local copies, waits for them, and re-layouts, attend(): values = key_values[:, :, model_width:].reshape(-1, H, head_size)  22.3 us
    while x24, local copies, waits for them, and re-layouts  21.4 us
    all_to_all x1, starting transfers between devices, body(): lax.all_to_all(request.reshape(slabs_n, per_owner), 'gz', split_axis=0, c...  19.2 us
  transfers between devices with their start and end apart: 3, of which 3 were waited for; matrix products, arithmetic and copies ran while one was open for 1% of the time, Pallas kernels for 0%

commit v1 on v0

--- a/solution.py
+++ b/solution.py
@@ -47,7 +47,12 @@
     projected = jnp.dot(normed, qkv_weight, preferred_element_type=jnp.float32).astype(jnp.bfloat16)
     queries = projected[:, :model_width].reshape(own_blocks, block_len, model_width)
     kv_own = projected[:, model_width:].reshape(own_blocks, block_len, 2 * model_width)
-    slab_kv = lax.all_gather(kv_own, "row", axis=0, tiled=True)
+    ring = [kv_own]
+    for hop in range(3):
+        ring.append(lax.ppermute(ring[-1], "row", [(dev, (dev + 1) % 4) for dev in range(4)]))
+    slab_kv = jnp.roll(
+        jnp.concatenate(ring[::-1], axis=0), (lax.axis_index("row") + 1) * ring[0].shape[0], axis=0
+    )
     owner_slab = key_blocks // slab_blocks
     within = key_blocks % slab_blocks
     slab_table = jnp.arange(slabs_n, dtype=jnp.int32)

time: 903 us -> 855 us (0.947)
  waiting for transfers between devices: 554 us -> 530 us
  matrix products: 48.5 us -> 29.6 us
  between operations: 13.5 us -> 0.25 us
  starting transfers between devices: 27 us -> 37 us
    all_gather x1 -> x0, waiting for transfers between devices: 46.3 us -> none  [body(): slab_kv = lax.all_gather(kv_own, 'row', axis=0, tiled=True)]
    ppermute x0 -> x3, waiting for transfers between devices: none -> 41.6 us  [body(): lax.ppermute(ring[-1], 'row', [(dev, (dev + 1) % 4) for dev in range(4)])]
    dot_general x8, matrix products: 25.1 us -> 5.77 us  [attend(): jnp.einsum('hqk,khd->qhd', weights.astype(jnp.bfloat16), values, preferre...]
    all_to_all x1, waiting for transfers between devices: 497 us -> 479 us  [body(): lax.all_to_all(kv_sent, 'gz', split_axis=0, concat_axis=0, tiled=True)]
    while x24, local copies, waits for them, and re-layouts: 21.4 us -> 10 us
    ppermute x0 -> x3, starting transfers between devices: none -> 10.4 us  [body(): lax.ppermute(ring[-1], 'row', [(dev, (dev + 1) % 4) for dev in range(4)])]
  transfers between devices with their start and end apart: 3 -> 5, of which waited for: 3 -> 5; matrix products, arithmetic and copies ran while one was open for 1% -> 2% of each run, Pallas kernels for 0% -> 0%
where the time goes in v1:
time: 855 us; the launch traced here: 851 us
  waiting for transfers between devices  530 us (62%)
  local copies, waits for them, and re-layouts  234 us (27%)
  starting transfers between devices  37 us (4%)
  matrix products  29.6 us (3%)
  other arithmetic  19.8 us (2%)
    all_to_all x1, waiting for transfers between devices, body(): lax.all_to_all(kv_sent, 'gz', split_axis=0, concat_axis=0, tiled=True)  479 us
    gather x16, local copies, waits for them, and re-layouts, one_block(): gathered = jnp.concatenate([slab_kv[near_row], far_kv[slot_row]], axis=0)  61.4 us
    slice x16, local copies, waits for them, and re-layouts, attend(): keys = key_values[:, :, :model_width].reshape(-1, H, head_size)  46.2 us
    ppermute x3, waiting for transfers between devices, body(): lax.ppermute(ring[-1], 'row', [(dev, (dev + 1) % 4) for dev in range(4)])  41.6 us
    slice x8, local copies, waits for them, and re-layouts, attend(): values = key_values[:, :, model_width:].reshape(-1, H, head_size)  22.3 us
    all_to_all x1, starting transfers between devices, body(): lax.all_to_all(request.reshape(slabs_n, per_owner), 'gz', split_axis=0, c...  19.2 us
    reshape x8, local copies, waits for them, and re-layouts, attend(): values = key_values[:, :, model_width:].reshape(-1, H, head_size)  19 us
    reshape x8, local copies, waits for them, and re-layouts, attend(): keys = key_values[:, :, :model_width].reshape(-1, H, head_size)  18.6 us
  transfers between devices with their start and end apart: 5, of which 5 were waited for; matrix products, arithmetic and copies ran while one was open for 2% of the time, Pallas kernels for 0%

profile of v1, /device:TPU:34, one launch (start us, length us, event | category | flops | bytes accessed | tf_op | source)
XLA Modules:
  0.0 850.8 jit_solution(8200928860401951791)
XLA Ops:
  3.8 19.2 %all-to-all-start = ((s32[128,1,1]{2,1,0:T(1,128)}), s32[128,1,1]{2,1,0:T(1,128)S(1)}, u32[]{:S(2)}, u32[]{:S(2)}) async-start(s32[128,1,1]{2,1,0:T(1,128)} %copy.48), calls=%async_computation | async-start | bytes 131072 | tf_op jit(solution)/shard_map/all_to_all | solution.py:71
  28.2 9.1 %all-to-all-done = s32[128,1,1]{2,1,0:T(1,128)S(1)} async-done(((s32[128,1,1]{2,1,0:T(1,128)}), s32[128,1,1]{2,1,0:T(1,128)S(1)}, u32[]{:S(2)}, u32[]{:S(2)}) %all-to-all-start) | async-done | bytes 544 | tf_op jit(solution)/shard_map/all_to_all | solution.py:71
  39.7 8.3 gather_fusion.2
  48.0 7.5 all-to-all-start.1
  55.5 3.4 collective-permute-start
  58.9 18.1 %collective-permute-done = bf16[8,64,768]{2,1,0:T(8,128)(2,1)S(1)} collective-permute-done((bf16[8,64,768]{2,1,0:T(8,128)(2,1)S(1)}, bf16[8,64,768]{2,1,0:T(8,128)(2,1)S(1)}, u32[]{:S(2)}, u32[]{:S(2)}) %collective-permute-start) | collective-permute-done | bytes 786464 | tf_op jit(solution)/shard_map/ppermute | solution.py:52
  76.9 3.4 collective-permute-start.1
  80.3 17.4 %collective-permute-done.1 = bf16[8,64,768]{2,1,0:T(8,128)(2,1)S(1)} collective-permute-done((bf16[8,64,768]{2,1,0:T(8,128)(2,1)S(1)}, bf16[8,64,768]{2,1,0:T(8,128)(2,1)S(1)}, u32[]{:S(2)}, u32[]{:S(2)}) %collective-permute-start.1) | collective-permute-done | bytes 786464 | tf_op jit(solution)/shard_map/ppermute | solution.py:52
  97.7 3.6 collective-permute-start.2
  112.8 6.2 collective-permute-done.2
  123.8 478.8 %all-to-all-done.1 = bf16[128,1,64,768]{3,2,1,0:T(8,128)(2,1)} async-done(((bf16[128,1,64,768]{3,2,1,0:T(8,128)(2,1)}), bf16[128,1,64,768]{3,2,1,0:T(8,128)(2,1)}, u32[]{:S(2)}, u32[]{:S(2)}) %all-to-all-start.1) | async-done | bytes 12582944 | tf_op jit(solution)/shard_map/all_to_all | solution.py:75
  602.6 242.0 %while.10 = (s32[]{:T(128)}, bf16[8,64,384]{2,1,0:T(8,128)(2,1)}, s32[8,4]{1,0:T(8,128)}, bf16[32,64,768]{2,1,0:T(8,128)(2,1)}, s32[8,16]{1,0:T(8,128)S(1)}, /*i...) while((s32[]{:T(128)}, bf16[8,64,384]{2,1,0:T(8,128)(2,1)}, ...), condition=%wide.region_8.9_spmd, body=%wide.region_5.8_spmd.sunk | while | flops 132760128 | bytes 37876240 | solution.py:85
  608.4 5.2 gather_fusion.1
  614.9 3.0 fusion.76
  638.6 5.2 gather_fusion.1
  645.1 3.0 fusion.76
  668.9 5.2 gather_fusion.1
  675.4 3.0 fusion.76
  699.1 5.2 gather_fusion.1
  729.4 5.2 gather_fusion.1
  759.6 5.2 gather_fusion.1
  789.9 5.2 gather_fusion.1
  820.1 5.2 gather_fusion.1
  846.4 3.5 fusion.29
  (239 shorter events, 221.0 us)
Async XLA Ops:
  0.0 846.3 %copy-start = (bf16[1536,384]{1,0:T(8,128)(2,1)S(1)}, bf16[1536,384]{1,0:T(8,128)(2,1)}, u32[]{:S(2)}) copy-start(bf16[1536,384]{1,0:T(8,128)(2,1)} %param.19) | copy-start | bytes 3538948
  1.6 0.9 copy-start.4
  2.9 0.9 copy-start.5
  3.8 33.5 %all-to-all-start = ((s32[128,1,1]{2,1,0:T(1,128)}), s32[128,1,1]{2,1,0:T(1,128)S(1)}, u32[]{:S(2)}, u32[]{:S(2)}) async-start(s32[128,1,1]{2,1,0:T(1,128)} %copy.48), calls=%async_computation | async-start | bytes 131072 | tf_op jit(solution)/shard_map/all_to_all | solution.py:71
  24.2 0.8 copy-start.2
  27.1 1.1 copy-start.3
  48.0 554.7 %all-to-all-start.1 = ((bf16[128,1,64,768]{3,2,1,0:T(8,128)(2,1)}), bf16[128,1,64,768]{3,2,1,0:T(8,128)(2,1)}, u32[]{:S(2)}, u32[]{:S(2)}) async-start(bf16[128,1,64,768]{3,2,1,0:T(8,128)(2,1)} %bitcast.77), calls=%async_computation.1 | async-start | bytes 25165824 | tf_op jit(solution)/shard_map/all_to_all | solution.py:75
  55.5 21.5 %collective-permute-start = (bf16[8,64,768]{2,1,0:T(8,128)(2,1)S(1)}, bf16[8,64,768]{2,1,0:T(8,128)(2,1)S(1)}, u32[]{:S(2)}, u32[]{:S(2)}) collective-permute-start(bf16[8,64,768]{2,1,0:T(8,128)(2,1)S(1)} %bitcast.74), channel_id=1, source_target_pairs={{0,1},{1,2},{2,3},{3,0},{4,5},{5,6},{6,7},{7,4},{8,9},{9,10},{10,1... | collective-permute-start | bytes 2359304 | tf_op jit(solution)/shard_map/ppermute | solution.py:52
  76.9 20.8 %collective-permute-start.1 = (bf16[8,64,768]{2,1,0:T(8,128)(2,1)S(1)}, bf16[8,64,768]{2,1,0:T(8,128)(2,1)S(1)}, u32[]{:S(2)}, u32[]{:S(2)}) collective-permute-start(bf16[8,64,768]{2,1,0:T(8,128)(2,1)S(1)} %collective-permute-done), channel_id=1, source_target_pairs={{0,1},{1,2},{2,3},{3,0},{4,5},{5,6},{6,7},{7,4},{8,9},{9,10},{10,1... | collective-permute-start | bytes 2359304 | tf_op jit(solution)/shard_map/ppermute | solution.py:52
  97.7 21.2 %collective-permute-start.2 = (bf16[8,64,768]{2,1,0:T(8,128)(2,1)S(1)}, bf16[8,64,768]{2,1,0:T(8,128)(2,1)}, u32[]{:S(2)}, u32[]{:S(2)}) collective-permute-start(bf16[8,64,768]{2,1,0:T(8,128)(2,1)S(1)} %collective-permute-done.1), channel_id=1, source_target_pairs={{0,1},{1,2},{2,3},{3,0},{4,5},{5,6},{6,7},{7,4},{8,9},{9,10},{10,1... | collective-permute-start | bytes 2359304 | tf_op jit(solution)/shard_map/ppermute | solution.py:52
  121.7 480.9 %copy-start.6 = (pred[8,20]{1,0:T(8,128)(4,1)S(1)}, pred[8,20]{1,0:T(8,128)(4,1)}, u32[]{:S(2)}) copy-start(pred[8,20]{1,0:T(8,128)(4,1)} %copy.51) | copy-start | bytes 484
  602.6 243.7 %copy-start.7 = (f32[384]{0:T(512)S(1)}, f32[384]{0:T(512)}, u32[]{:S(2)}) copy-start(f32[384]{0:T(512)} %param.17) | copy-start | bytes 4612
  630.2 1.2 copy-start.1
  660.5 1.2 copy-start.1
  690.7 1.2 copy-start.1
  721.0 1.2 copy-start.1
  751.3 1.2 copy-start.1
  781.5 1.2 copy-start.1
  811.8 1.2 copy-start.1
  842.0 1.2 copy-start.1
